TPU v7x, 512 devices: a whole 4x4x16 slice. The times are simulated.
512 devices in a mesh: ctx: 64 (over y, z_hi, x, core), head: 8 (over z_lo).
Axes of the slice: x: 4, y: 4, z: 16 (z_hi: 2, z_lo: 8; z = z_hi * 8 + z_lo), core: 2. Of those that a mesh axis runs over, the one named last changes fastest.
Arguments:
- query_raw: bfloat16 [16384, 5120], P('ctx', 'head'), may hold values from -9 to 9
- key_raw: bfloat16 [16384, 5120], P('ctx', 'head'), may hold values from -9 to 9
- values: bfloat16 [16384, 5120], P('ctx', 'head'), may hold values from -6 to 6
- out_grad: bfloat16 [16384, 5120], P('ctx', 'head'), may hold values from -128 to 128
- query_gain: float32 [5120], P('head'), may hold values from 0.25 to 1.75
- key_gain: float32 [5120], P('head'), may hold values from 0.25 to 1.75
- key_tiles: int32 [128, 4], P('ctx'), may hold values from 0 to 127, as said below
- global_ids: int32 [128], P('ctx'), may hold values from 0 to 16383, as said below
- readers: int32 [64, 64], P('ctx'), may hold values from 0 to 1, as said below
Outputs:
- query_grad: bfloat16 [16384, 5120], P('ctx', 'head')
- key_grad: bfloat16 [16384, 5120], P('ctx', 'head')
- value_grad: bfloat16 [16384, 5120], P('ctx', 'head')
Inputs may be any that keep to these rules, and one draw needn't show every extreme that they name: `key_tiles`: row t lists, ascending, the 4 tiles of 4 consecutive tile-frames of 1 tiles; every listed tile lies on an index of ctx at most 1 away from tile t's, and in every draw some tile reads a tile exactly 1 below and some tile one exactly 1 above. `global_ids`: entries c * 2 to (c + 1) * 2 - 1 are distinct ascending tokens of index c of ctx. `readers`: each row has either one 1 or all 64 entries 1; at least one row has all.
All inputs are finite; a program needn't handle non-finite values.
Results may differ from a plain program's by a relative error of at most 0.02.
Values may be sent and summed in bfloat16 or wider, within the bound.
A program may use at most 64 MiB of HBM per device.

v0:
```python
import jax
import jax.numpy as jnp
from jax import lax
from jax.sharding import PartitionSpec as P

HEAD_DIM = 128
D = 5120
TILE = 128
REACH = 1
G_DEV = 2
EPSILON = 1e-06


def passed_along(shard, axis, by):
    count = lax.axis_size(axis)
    return lax.ppermute(shard, axis, [(i, (i + by) % count) for i in range(count)])


def normalize(as_float, gain, squares):
    inverse = lax.rsqrt(squares[:, None] / D + EPSILON)
    return (inverse, (as_float * inverse * gain).astype(jnp.bfloat16))


def norm_grad(as_float, inverse, scaled, coeffs):
    return (inverse * scaled - as_float * inverse**3 * (coeffs[:, None] / D)).astype(jnp.bfloat16)


def body(
    query_raw, key_raw, values, out_grad, query_gain, key_gain, key_tiles, global_ids, readers
):
    tokens_here, width_here = query_raw.shape
    heads_here = width_here // HEAD_DIM
    tiles_here = tokens_here // TILE
    factor = HEAD_DIM ** (-0.5)
    device = lax.axis_index("ctx")
    query_rows = query_raw.astype(jnp.float32)
    key_rows = key_raw.astype(jnp.float32)
    query_sq, key_sq = lax.psum(
        (jnp.sum(query_rows * query_rows, axis=1), jnp.sum(key_rows * key_rows, axis=1)), "head"
    )
    query_inv, query_norm = normalize(query_rows, query_gain, query_sq)
    key_inv, key_norm = normalize(key_rows, key_gain, key_sq)
    own_rows = global_ids - device * tokens_here
    own_pair = jnp.stack([key_norm[own_rows], values[own_rows]])
    global_pair = lax.all_gather(own_pair, "ctx", axis=1, tiled=True)
    global_keys = global_pair[0].reshape(-1, heads_here, HEAD_DIM)
    global_vals = global_pair[1].reshape(-1, heads_here, HEAD_DIM)
    live_mask = jnp.repeat(readers[0] > 0, G_DEV)
    key_value = jnp.stack([key_norm, values])
    current = passed_along(key_value, "ctx", -REACH)
    pieces = [current]
    for hop_index in range(2 * REACH):
        current = passed_along(current, "ctx", 1)
        pieces.append(current)
    pieces = pieces[::-1]
    window_pair = jnp.concatenate(pieces, axis=1)
    first_tile = (device - REACH) * tiles_here
    local_tiles = key_tiles - first_tile
    window_rows = (
        local_tiles[:, :, None] * TILE + jnp.arange(TILE, dtype=jnp.int32)[None, None, :]
    ).reshape(tiles_here, -1)
    window_count = window_rows.shape[1]
    window_keys = window_pair[0][window_rows].reshape(
        tiles_here, window_count, heads_here, HEAD_DIM
    )
    window_vals = window_pair[1][window_rows].reshape(
        tiles_here, window_count, heads_here, HEAD_DIM
    )
    query_four = query_norm.reshape(tiles_here, TILE, heads_here, HEAD_DIM)
    grad_four = out_grad.reshape(tiles_here, TILE, heads_here, HEAD_DIM)

    def head_block(head_number):
        query_head = lax.dynamic_index_in_dim(query_four, head_number, 2, keepdims=False)
        grad_head = lax.dynamic_index_in_dim(grad_four, head_number, 2, keepdims=False)
        wkeys = lax.dynamic_index_in_dim(window_keys, head_number, 2, keepdims=False)
        wvals = lax.dynamic_index_in_dim(window_vals, head_number, 2, keepdims=False)
        gkeys = lax.dynamic_index_in_dim(global_keys, head_number, 1, keepdims=False)
        gvals = lax.dynamic_index_in_dim(global_vals, head_number, 1, keepdims=False)
        score_window = (
            jnp.einsum("tqd,tkd->tqk", query_head, wkeys, preferred_element_type=jnp.float32)
            * factor
        )
        score_global = (
            jnp.einsum("tqd,kd->tqk", query_head, gkeys, preferred_element_type=jnp.float32)
            * factor
        )
        score_global = jnp.where(live_mask, score_global, -jnp.inf)
        scores = jnp.concatenate([score_window, score_global], axis=2)
        largest = jnp.max(scores, axis=2, keepdims=True)
        log_total = largest + jnp.log(jnp.sum(jnp.exp(scores - largest), axis=2, keepdims=True))
        probs = jnp.exp(scores - log_total)
        probs_low = probs.astype(jnp.bfloat16)
        attended = jnp.einsum(
            "tqk,tkd->tqd", probs_low[..., :window_count], wvals, preferred_element_type=jnp.float32
        )
        attended = attended + jnp.einsum(
            "tqk,kd->tqd", probs_low[..., window_count:], gvals, preferred_element_type=jnp.float32
        )
        attended = lax.optimization_barrier(attended.astype(jnp.bfloat16))
        delta_rows = jnp.sum(grad_head.astype(jnp.float32) * attended.astype(jnp.float32), axis=2)
        dprob = jnp.concatenate(
            [
                jnp.einsum("tqd,tkd->tqk", grad_head, wvals, preferred_element_type=jnp.float32),
                jnp.einsum("tqd,kd->tqk", grad_head, gvals, preferred_element_type=jnp.float32),
            ],
            axis=2,
        )
        dscore = (probs * (dprob - delta_rows[..., None]) * factor).astype(jnp.bfloat16)
        grad_query = jnp.einsum(
            "tqk,tkd->tqd", dscore[..., :window_count], wkeys, preferred_element_type=jnp.float32
        )
        grad_query = grad_query + jnp.einsum(
            "tqk,kd->tqd", dscore[..., window_count:], gkeys, preferred_element_type=jnp.float32
        )
        window_dk = jnp.einsum(
            "tqk,tqd->tkd",
            dscore[..., :window_count],
            query_head,
            preferred_element_type=jnp.float32,
        )
        window_dv = jnp.einsum(
            "tqk,tqd->tkd",
            probs_low[..., :window_count],
            grad_head,
            preferred_element_type=jnp.float32,
        )
        global_dk = jnp.einsum(
            "tqk,tqd->kd",
            dscore[..., window_count:],
            query_head,
            preferred_element_type=jnp.float32,
        )
        global_dv = jnp.einsum(
            "tqk,tqd->kd",
            probs_low[..., window_count:],
            grad_head,
            preferred_element_type=jnp.float32,
        )
        return (grad_query, window_dk, window_dv, global_dk, global_dv)

    head_results = lax.map(head_block, jnp.arange(heads_here, dtype=jnp.int32))
    grad_query = jnp.moveaxis(head_results[0], 0, 2).reshape(tokens_here, width_here)
    window_dk = jnp.moveaxis(head_results[1], 0, 2).reshape(-1, width_here)
    window_dv = jnp.moveaxis(head_results[2], 0, 2).reshape(-1, width_here)
    global_dk = jnp.moveaxis(head_results[3], 0, 1).reshape(-1, width_here)
    global_dv = jnp.moveaxis(head_results[4], 0, 1).reshape(-1, width_here)
    window_grads = jnp.zeros((2, window_pair.shape[1], width_here), jnp.float32)
    window_grads = window_grads.at[:, window_rows.reshape(-1)].add(
        jnp.stack([window_dk, window_dv])
    )
    spread_grads = window_grads.reshape(2, 2 * REACH + 1, tokens_here, width_here)
    slots = [spread_grads[:, slot_index] for slot_index in range(2 * REACH + 1)]
    carried = slots[2 * REACH]
    for hop_index in range(2 * REACH):
        carried = (
            passed_along(carried.astype(jnp.bfloat16), "ctx", 1).astype(carried.dtype)
            + slots[2 * REACH - 1 - hop_index]
        )
    home_grads = passed_along(carried.astype(jnp.bfloat16), "ctx", -REACH).astype(carried.dtype)
    global_part = lax.psum_scatter(
        jnp.stack([global_dk, global_dv]), "ctx", scatter_dimension=1, tiled=True
    )
    home_grads = home_grads.at[:, own_rows].add(global_part)
    scaled_query = grad_query * query_gain
    scaled_key = home_grads[0] * key_gain
    query_dot, key_dot = lax.psum(
        (jnp.sum(scaled_query * query_rows, axis=1), jnp.sum(scaled_key * key_rows, axis=1)), "head"
    )
    query_grad = norm_grad(query_rows, query_inv, scaled_query, query_dot)
    key_grad = norm_grad(key_rows, key_inv, scaled_key, key_dot)
    return (query_grad, key_grad, home_grads[1].astype(jnp.bfloat16))


def solution(mesh):
    return jax.shard_map(
        body,
        mesh=mesh,
        in_specs=(
            P("ctx", "head"),
            P("ctx", "head"),
            P("ctx", "head"),
            P("ctx", "head"),
            P("head"),
            P("head"),
            P("ctx", None),
            P("ctx"),
            P("ctx", None),
        ),
        out_specs=(P("ctx", "head"), P("ctx", "head"), P("ctx", "head")),
        check_vma=False,
    )
```

profile of v0, /device:TPU:0, one launch (start us, length us, event | category | flops | bytes accessed | tf_op | source)
XLA Modules:
  0.0 1697.6 jit_solution(5765392369090235249)
XLA Ops:
  7.3 1.2 copy.58
  8.6 1.1 fusion.75
  9.7 30.9 %all-reduce.2 = (f32[256]{0:T(256)S(1)}, f32[256]{0:T(256)S(1)}) all-reduce(f32[256]{0:T(256)S(1)} %fusion.68, f32[256]{0:T(256)S(1)} %fusion.75), channel_id=1, replica_groups=mesh['ctx'=64,'head'=8] {'head'}, use_global_device_ids=true, to_apply=%region_1.0 | all-reduce | flops 512 | bytes 4096 | tf_op jit(solution)/shard_map/psum | solution.py:38
  41.2 1.1 fusion.88
  42.5 8.5 collective-permute-start
  53.0 8.4 collective-permute-done
  61.4 1.9 collective-permute-start.1
  63.4 166.6 %all_gather.3 = bf16[2,128,640]{2,0,1:T(2,128)(2,1)S(1)} all-gather(bf16[2,2,640]{2,0,1:T(2,128)(2,1)S(1)} %copy.60), channel_id=1, replica_groups=mesh['ctx'=64,'head'=8] {'ctx'}, dimensions={1}, use_global_device_ids=true | all-gather | bytes 332800 | tf_op jit(solution)/shard_map/all_gather | solution.py:45
  233.7 2.4 collective-permute-start.2
  237.4 27.7 %collective-permute-done.2 = bf16[2,256,640]{2,1,0:T(8,128)(2,1)S(1)} collective-permute-done((bf16[2,256,640]{2,1,0:T(8,128)(2,1)S(1)}, bf16[2,256,640]{2,1,0:T(8,128)(2,1)S(1)}, u32[]{:S(2)}, u32[]{:S(2)}) %collective-permute-start.2) | collective-permute-done | bytes 655392 | tf_op jit(solution)/shard_map/ppermute | solution.py:16
  265.6 5.2 gather_fusion
  270.8 4.1 reshape.218
  274.9 1.8 copy.66
  276.7 5.2 gather_fusion.3
  281.9 4.1 reshape.220
  286.0 1.8 copy.69
  287.8 76.5 %while.19 = (s32[]{:T(128)}, f32[5,2,128,128]{3,2,1,0:T(8,128)}, f32[5,2,512,128]{3,2,1,0:T(8,128)}, f32[5,2,512,128]{3,2,1,0:T(8,128)}, f32[5,128,128]{1,2,0:T(...) while((s32[]{:T(128)}, f32[5,2,128,128]{3,2,1,0:T(8,128)}, ...), condition=%wide.region_9.10_spmd.clone, body=%wide.region_4.9_spmd.clone.sunk | while | flops 254377472 | bytes 9916299 | solution.py:141
  293.3 1.0 fusion.145
  294.8 0.9 fusion.148
  297.4 1.1 fusion.153
  298.5 1.1 fusion.154
  299.6 0.9 fusion.151
  308.6 1.0 fusion.145
  310.1 0.9 fusion.148
  312.7 1.1 fusion.153
  313.8 1.1 fusion.154
  314.9 0.9 fusion.151
  323.9 1.0 fusion.145
  325.3 0.9 fusion.148
  328.0 1.1 fusion.153
  329.1 1.1 fusion.154
  330.2 0.9 fusion.151
  339.2 1.0 fusion.145
  340.6 0.9 fusion.148
  343.3 1.1 fusion.153
  344.4 1.1 fusion.154
  354.5 1.0 fusion.145
  355.9 0.9 fusion.148
  358.6 1.1 fusion.153
  359.7 1.1 fusion.154
  364.3 5.1 copy.72
  369.3 3.7 stack_reshape.12
  373.0 5.1 copy.73
  378.1 4.8 stack_reshape.13
  383.0 4.7 maximum_bitcast_fusion
  387.7 8.8 copy.74
  396.5 3.0 broadcast_in_dim.59
  399.4 131.0 %scatter_fusion = f32[2,768,640]{2,0,1:T(2,128)} fusion(f32[2,768,640]{2,0,1:T(2,128)} %broadcast_in_dim.59, s32[1024]{0:T(1024)S(1)} %bitcast.214, f32[1024,2,640]{2,1,0:T(2,128)} %copy.74), kind=kCustom, calls=%fused_computation.4 | custom fusion | flops 1310720 | bytes 15732736 | tf_op jit(solution)/shard_map/scatter-add | solution.py:148
  530.4 1.8 fusion.82
  532.3 1.9 collective-permute-start.3
  534.2 24.1 %collective-permute-done.3 = bf16[2,256,640]{2,0,1:T(2,128)(2,1)S(1)} collective-permute-done((bf16[2,256,640]{2,0,1:T(2,128)(2,1)S(1)}, bf16[2,256,640]{2,0,1:T(2,128)(2,1)S(1)}, u32[]{:S(2)}, u32[]{:S(2)}) %collective-permute-start.3) | collective-permute-done | bytes 655392 | tf_op jit(solution)/shard_map/ppermute | solution.py:16
  558.3 2.0 fusion.67
  560.3 2.1 collective-permute-start.4
  562.5 1.0 pad_maximum_fusion.2
  563.5 1.2 copy.77
  564.8 20.6 %collective-permute-done.4 = bf16[2,256,640]{2,0,1:T(2,128)(2,1)S(1)} collective-permute-done((bf16[2,256,640]{2,0,1:T(2,128)(2,1)S(1)}, bf16[2,256,640]{2,0,1:T(2,128)(2,1)S(1)}, u32[]{:S(2)}, u32[]{:S(2)}) %collective-permute-start.4) | collective-permute-done | bytes 655392 | tf_op jit(solution)/shard_map/ppermute | solution.py:16
  585.4 2.0 fusion.65
  587.4 1.9 collective-permute-start.5
  589.3 1.3 dynamic-slice
  592.3 1057.7 %all-reduce.5.cloned.1.call-done = f32[2,128,640]{2,0,1:T(2,128)} async-done(((f32[2,128,640]{2,0,1:T(2,128)}), f32[2,128,640]{2,0,1:T(2,128)}) %all-reduce.5.cloned.1.call-update) | async-done | bytes 655376
  1650.7 1.6 convert_element_type.66
  1653.4 1.5 slice.111
  1655.1 32.8 %all-reduce.1 = (f32[256]{0:T(256)S(1)}, f32[256]{0:T(256)S(1)}) all-reduce(f32[256]{0:T(256)S(1)} %fusion.74, f32[256]{0:T(256)S(1)} %fusion.81), channel_id=1, replica_groups=mesh['ctx'=64,'head'=8] {'head'}, use_global_device_ids=true, to_apply=%region_11.12 | all-reduce | flops 512 | bytes 4096 | tf_op jit(solution)/shard_map/psum | solution.py:166
  1689.8 0.9 fusion.80
  (211 shorter events, 55.7 us)
Async XLA Ops:
  7.2 45.1 %copy-start = (bf16[256,640]{1,0:T(8,128)(2,1)S(1)}, bf16[256,640]{1,0:T(8,128)(2,1)}, u32[]{:S(2)}) copy-start(bf16[256,640]{1,0:T(8,128)(2,1)} %param.12) | copy-start | bytes 983044
  7.2 45.1 %copy-start.9 = (f32[640]{0:T(1024)S(1)}, f32[640]{0:T(1024)}, u32[]{:S(2)}) copy-start(f32[640]{0:T(1024)} %param.16) | copy-start | bytes 7684
  7.2 35.2 %copy-start.6 = (bf16[256,640]{1,0:T(8,128)(2,1)S(1)}, bf16[256,640]{1,0:T(8,128)(2,1)}, u32[]{:S(2)}) copy-start(bf16[256,640]{1,0:T(8,128)(2,1)} %param.13) | copy-start | bytes 983044
  7.2 43.9 %copy-start.21 = (s32[2,4]{1,0:T(2,128)S(1)}, s32[2,4]{1,0:T(2,128)}, u32[]{:S(2)}) copy-start(s32[2,4]{1,0:T(2,128)} %param.17) | copy-start | bytes 100
  7.2 44.0 %copy-start.22 = (s32[2]{0:T(128)S(1)}, s32[2]{0:T(128)}, u32[]{:S(2)}) copy-start(s32[2]{0:T(128)} %param.18) | copy-start | bytes 28
  7.2 1642.8 %all-reduce.5.cloned.1.call-start = ((), (), s32[]{:S(2)}) async-start(), calls=%async_computation | async-start | bytes 1310720
  8.5 223.8 %copy-start.2 = (bf16[256,640]{0,1:T(8,128)(2,1)}, bf16[256,640]{0,1:T(8,128)(2,1)S(1)}, u32[]{:S(2)}) copy-start(bf16[256,640]{0,1:T(8,128)(2,1)S(1)} %copy.58) | copy-start | bytes 983044
  41.2 22.1 %copy-start.13 = (f32[256]{0:T(256)}, f32[256]{0:T(256)S(1)}, u32[]{:S(2)}) copy-start(f32[256]{0:T(256)S(1)} %get-tuple-element.204) | copy-start | bytes 3076
  41.2 191.0 %copy-start.15 = (f32[256]{0:T(256)}, f32[256]{0:T(256)S(1)}, u32[]{:S(2)}) copy-start(f32[256]{0:T(256)S(1)} %get-tuple-element.207) | copy-start | bytes 3076
  42.5 189.8 %copy-start.10 = (f32[640]{0:T(1024)S(1)}, f32[640]{0:T(1024)}, u32[]{:S(2)}) copy-start(f32[640]{0:T(1024)} %param.15) | copy-start | bytes 7684
  42.5 18.9 %collective-permute-start = (bf16[2,256,640]{2,1,0:T(8,128)(2,1)S(1)}, bf16[2,256,640]{2,1,0:T(8,128)(2,1)S(1)}, u32[]{:S(2)}, u32[]{:S(2)}) collective-permute-start(bf16[2,256,640]{2,1,0:T(8,128)(2,1)S(1)} %pad_maximum_fusion.1), channel_id=1, source_target_pairs={{0,504},{8,0},{16,8},{24,16},{32,24},{40,32},{48,40},{56,48},{64,5... | collective-permute-start | bytes 1966088 | tf_op jit(solution)/shard_map/ppermute | solution.py:16
  51.2 0.5 copy-start.19
  61.4 172.3 %collective-permute-start.1 = (bf16[2,256,640]{2,1,0:T(8,128)(2,1)S(1)}, bf16[2,256,640]{2,1,0:T(8,128)(2,1)S(1)}, u32[]{:S(2)}, u32[]{:S(2)}) collective-permute-start(bf16[2,256,640]{2,1,0:T(8,128)(2,1)S(1)} %collective-permute-done), channel_id=1, source_target_pairs={{0,8},{8,16},{16,24},{24,32},{32,40},{40,48},{48,56},{56,64},{64,7... | collective-permute-start | bytes 1966088 | tf_op jit(solution)/shard_map/ppermute | solution.py:16
  63.4 169.9 %copy-start.8 = (bf16[256,640]{1,0:T(8,128)(2,1)S(1)}, bf16[256,640]{1,0:T(8,128)(2,1)}, u32[]{:S(2)}) copy-start(bf16[256,640]{1,0:T(8,128)(2,1)} %param.14) | copy-start | bytes 983044
  230.5 5.7 copy-start.23
  233.7 31.4 %collective-permute-start.2 = (bf16[2,256,640]{2,1,0:T(8,128)(2,1)S(1)}, bf16[2,256,640]{2,1,0:T(8,128)(2,1)S(1)}, u32[]{:S(2)}, u32[]{:S(2)}) collective-permute-start(bf16[2,256,640]{2,1,0:T(8,128)(2,1)S(1)} %collective-permute-done.1), channel_id=1, source_target_pairs={{0,8},{8,16},{16,24},{24,32},{32,40},{40,48},{48,56},{56,64},{64,7... | collective-permute-start | bytes 1966088 | tf_op jit(solution)/shard_map/ppermute | solution.py:16
  287.8 4.0 copy-start.24
  297.4 5.7 copy-start.25
  303.1 4.0 copy-start.24
  312.7 5.7 copy-start.25
  318.4 4.0 copy-start.24
  328.0 5.7 copy-start.25
  333.7 4.0 copy-start.24
  343.3 5.7 copy-start.25
  349.0 4.0 copy-start.24
  358.6 5.7 copy-start.25
  396.5 3.0 copy-start.12
  530.4 32.0 %copy-start.7 = (f32[5,128,128]{1,2,0:T(8,128)S(1)}, f32[5,128,128]{1,2,0:T(8,128)}, u32[]{:S(2)}) copy-start(f32[5,128,128]{1,2,0:T(8,128)} %get-tuple-element.82) | copy-start | bytes 983044
  532.3 26.0 %collective-permute-start.3 = (bf16[2,256,640]{2,0,1:T(2,128)(2,1)S(1)}, bf16[2,256,640]{2,0,1:T(2,128)(2,1)S(1)}, u32[]{:S(2)}, u32[]{:S(2)}) collective-permute-start(bf16[2,256,640]{2,0,1:T(2,128)(2,1)S(1)} %fusion.82), channel_id=1, source_target_pairs={{0,8},{8,16},{16,24},{24,32},{32,40},{40,48},{48,56},{56,64},{64,7... | collective-permute-start | bytes 1966088 | tf_op jit(solution)/shard_map/ppermute | solution.py:16
  560.3 25.0 %collective-permute-start.4 = (bf16[2,256,640]{2,0,1:T(2,128)(2,1)S(1)}, bf16[2,256,640]{2,0,1:T(2,128)(2,1)S(1)}, u32[]{:S(2)}, u32[]{:S(2)}) collective-permute-start(bf16[2,256,640]{2,0,1:T(2,128)(2,1)S(1)} %fusion.67), channel_id=1, source_target_pairs={{0,8},{8,16},{16,24},{24,32},{32,40},{40,48},{48,56},{56,64},{64,7... | collective-permute-start | bytes 1966088 | tf_op jit(solution)/shard_map/ppermute | solution.py:16
  564.8 26.5 %copy-start.5 = (f32[5,2,128,128]{3,2,1,0:T(8,128)S(1)}, f32[5,2,128,128]{3,2,1,0:T(8,128)}, u32[]{:S(2)}) copy-start(f32[5,2,128,128]{3,2,1,0:T(8,128)} %get-tuple-element.79) | copy-start | bytes 1966084
  564.8 27.4 %copy-start.3 = (bf16[256,640]{0,1:T(8,128)(2,1)S(1)}, bf16[256,640]{0,1:T(8,128)(2,1)}, u32[]{:S(2)}) copy-start(bf16[256,640]{0,1:T(8,128)(2,1)} %copy-done.2) | copy-start | bytes 983044
  564.8 27.4 %copy-start.11 = (f32[640]{0:T(1024)S(1)}, f32[640]{0:T(1024)}, u32[]{:S(2)}) copy-start(f32[640]{0:T(1024)} %param.15) | copy-start | bytes 7684
  587.4 1063.4 %collective-permute-start.5 = (bf16[2,256,640]{2,0,1:T(2,128)(2,1)S(1)}, bf16[2,256,640]{2,0,1:T(2,128)(2,1)}, u32[]{:S(2)}, u32[]{:S(2)}) collective-permute-start(bf16[2,256,640]{2,0,1:T(2,128)(2,1)S(1)} %fusion.65), channel_id=1, source_target_pairs={{0,504},{8,0},{16,8},{24,16},{32,24},{40,32},{48,40},{56,48},{64,5... | collective-permute-start | bytes 1966088 | tf_op jit(solution)/shard_map/ppermute | solution.py:16
  591.2 1061.1 %copy-start.20 = (s32[2]{0:T(128)S(1)}, s32[2]{0:T(128)}, u32[]{:S(2)}) copy-start(s32[2]{0:T(128)} %copy-done.19) | copy-start | bytes 28
  1650.7 4.2 copy-start.1
  1652.3 35.7 %copy-start.16 = (f32[256]{0:T(256)S(1)}, f32[256]{0:T(256)}, u32[]{:S(2)}) copy-start(f32[256]{0:T(256)} %copy-done.15) | copy-start | bytes 3076
  1652.3 35.7 %copy-start.18 = (f32[256]{0:T(256)S(1)}, f32[256]{0:T(256)}, u32[]{:S(2)}) copy-start(f32[256]{0:T(256)} %get-tuple-element.208) | copy-start | bytes 3076
  1655.0 34.1 %copy-start.4 = (bf16[1,256,640]{2,0,1:T(2,128)(2,1)S(1)}, bf16[1,256,640]{2,0,1:T(2,128)(2,1)}, u32[]{:S(2)}) copy-start(bf16[1,256,640]{2,0,1:T(2,128)(2,1)} %slice.111) | copy-start | bytes 983044
  1655.0 34.9 %copy-start.14 = (f32[256]{0:T(256)S(1)}, f32[256]{0:T(256)}, u32[]{:S(2)}) copy-start(f32[256]{0:T(256)} %copy-done.13) | copy-start | bytes 3076
  1655.0 34.9 %copy-start.17 = (f32[256]{0:T(256)S(1)}, f32[256]{0:T(256)}, u32[]{:S(2)}) copy-start(f32[256]{0:T(256)} %get-tuple-element.203) | copy-start | bytes 3076
Sparse Core Ops, SparseCore 0:
  564.9 1085.0 all-reduce.4
where the time goes:
time: 1700 us
  waiting for transfers between devices  1140 us (67%)
  blocking collectives  230 us (14%)
  other arithmetic  153 us (9%)
  local copies, waits for them, and re-layouts  84.9 us (5%)
  matrix products  46.1 us (3%)
  starting transfers between devices  18.9 us (1%)
    unnamed x2, waiting for transfers between devices  1060 us
    all_gather x1, blocking collectives, body(): global_pair = lax.all_gather(own_pair, 'ctx', axis=1, tiled=True)  167 us
    scatter-add x1, other arithmetic, body(): window_grads.at[:, window_rows.reshape(-1)]  131 us
    ppermute x6, waiting for transfers between devices, passed_along(): lax.ppermute(shard, axis, [(i, (i + by) % count) for i in range(count)])  80.8 us
  transfers between devices with their start and end apart: 7, of which 5 were waited for; matrix products, arithmetic and copies ran while one was open for 1% of the time, Pallas kernels for 0%

commit v1 on v0

--- a/solution.py
+++ b/solution.py
@@ -2,6 +2,7 @@
 import jax.numpy as jnp
 from jax import lax
 from jax.sharding import PartitionSpec as P
+from jax.lax import all_to_all, psum
 
 HEAD_DIM = 128
 D = 5120
@@ -42,7 +43,10 @@
     key_inv, key_norm = normalize(key_rows, key_gain, key_sq)
     own_rows = global_ids - device * tokens_here
     own_pair = jnp.stack([key_norm[own_rows], values[own_rows]])
-    global_pair = lax.all_gather(own_pair, "ctx", axis=1, tiled=True)
+    made = []
+    for _ in range(psum(1, "ctx")):
+        made.append(own_pair)
+    global_pair = jnp.concatenate(all_to_all(jnp.stack(made, axis=0), "ctx", 0, 0), axis=1)
     global_keys = global_pair[0].reshape(-1, heads_here, HEAD_DIM)
     global_vals = global_pair[1].reshape(-1, heads_here, HEAD_DIM)
     live_mask = jnp.repeat(readers[0] > 0, G_DEV)

time: 1700 us -> 1580 us (0.929)
  blocking collectives: 230 us -> 63.8 us
  waiting for transfers between devices: 1140 us -> 1170 us
    all_gather x1 -> x0, blocking collectives: 167 us -> none  [body(): global_pair = lax.all_gather(own_pair, 'ctx', axis=1, tiled=True)]
    ppermute x6, waiting for transfers between devices: 80.8 us -> 113 us  [passed_along(): lax.ppermute(shard, axis, [(i, (i + by) % count) for i in range(count)])]
  transfers between devices with their start and end apart: 7 -> 8, of which waited for: 5 -> 6; matrix products, arithmetic and copies ran while one was open for 1% -> 1% of each run, Pallas kernels for 0% -> 0%
where the time goes in v1:
time: 1580 us; the launch traced here: 1570 us
  waiting for transfers between devices  1170 us (74%)
  other arithmetic  153 us (10%)
  local copies, waits for them, and re-layouts  85.4 us (5%)
  blocking collectives  63.8 us (4%)
  matrix products  46.2 us (3%)
  starting transfers between devices  25.7 us (2%)
    unnamed x2, waiting for transfers between devices  1060 us
    scatter-add x1, other arithmetic, body(): window_grads.at[:, window_rows.reshape(-1)]  131 us
    ppermute x6, waiting for transfers between devices, passed_along(): lax.ppermute(shard, axis, [(i, (i + by) % count) for i in range(count)])  113 us
    psum x1, blocking collectives, body(): lax.psum((jnp.sum(scaled_query * query_rows, axis=1), jnp.sum(scaled_key...  32.8 us
  transfers between devices with their start and end apart: 8, of which 6 were waited for; matrix products, arithmetic and copies ran while one was open for 1% of the time, Pallas kernels for 0%

profile of v1, /device:TPU:0, one launch (start us, length us, event | category | flops | bytes accessed | tf_op | source)
XLA Modules:
  0.0 1570.4 jit_solution(3217866990400071710)
XLA Ops:
  7.2 1.2 copy.54
  8.6 1.1 fusion.75
  9.7 30.9 %all-reduce.2 = (f32[256]{0:T(256)S(1)}, f32[256]{0:T(256)S(1)}) all-reduce(f32[256]{0:T(256)S(1)} %fusion.68, f32[256]{0:T(256)S(1)} %fusion.75), channel_id=1, replica_groups=mesh['ctx'=64,'head'=8] {'head'}, use_global_device_ids=true, to_apply=%region_1.0 | all-reduce | flops 512 | bytes 4096 | tf_op jit(solution)/shard_map/psum | solution.py:39
  41.2 1.1 fusion.88
  42.5 8.5 collective-permute-start
  53.1 0.9 stack.24
  54.0 7.2 all-to-all-start
  61.3 3.5 collective-permute-done
  64.8 1.9 collective-permute-start.1
  68.3 32.5 %collective-permute-done.1 = bf16[2,256,640]{2,1,0:T(8,128)(2,1)S(1)} collective-permute-done((bf16[2,256,640]{2,1,0:T(8,128)(2,1)S(1)}, bf16[2,256,640]{2,1,0:T(8,128)(2,1)S(1)}, u32[]{:S(2)}, u32[]{:S(2)}) %collective-permute-start.1) | collective-permute-done | bytes 655392 | tf_op jit(solution)/shard_map/ppermute | solution.py:17
  100.8 2.1 collective-permute-start.2
  105.9 28.8 %collective-permute-done.2 = bf16[2,256,640]{2,1,0:T(8,128)(2,1)S(1)} collective-permute-done((bf16[2,256,640]{2,1,0:T(8,128)(2,1)S(1)}, bf16[2,256,640]{2,1,0:T(8,128)(2,1)S(1)}, u32[]{:S(2)}, u32[]{:S(2)}) %collective-permute-start.2) | collective-permute-done | bytes 655392 | tf_op jit(solution)/shard_map/ppermute | solution.py:17
  135.2 5.2 gather_fusion
  140.4 4.1 reshape.229
  144.5 1.8 copy.59
  146.3 5.2 gather_fusion.3
  151.5 4.1 reshape.231
  155.6 1.8 copy.62
  157.4 76.4 %while.19 = (s32[]{:T(128)}, f32[5,2,128,128]{3,2,1,0:T(8,128)}, f32[5,2,512,128]{3,2,1,0:T(8,128)}, f32[5,2,512,128]{3,2,1,0:T(8,128)}, f32[5,128,128]{1,2,0:T(...) while((s32[]{:T(128)}, f32[5,2,128,128]{3,2,1,0:T(8,128)}, ...), condition=%wide.region_9.10_spmd.clone, body=%wide.region_4.9_spmd.clone.sunk | while | flops 254377472 | bytes 9916299 | solution.py:145
  162.9 1.0 fusion.145
  164.4 0.9 fusion.148
  165.9 0.9 fusion.143
  167.1 1.1 fusion.153
  168.1 1.1 fusion.154
  178.2 1.0 fusion.145
  181.2 0.9 fusion.143
  182.3 1.1 fusion.153
  183.4 1.1 fusion.154
  193.5 1.0 fusion.145
  196.4 0.9 fusion.143
  197.6 1.1 fusion.153
  198.7 1.1 fusion.154
  208.7 1.0 fusion.145
  211.7 0.9 fusion.143
  212.9 1.1 fusion.153
  213.9 1.1 fusion.154
  224.0 1.0 fusion.145
  227.0 0.9 fusion.143
  228.1 1.1 fusion.153
  229.2 1.1 fusion.154
  233.8 5.1 copy.65
  238.9 3.7 stack_reshape.12
  242.6 5.1 copy.66
  247.7 4.8 stack_reshape.13
  252.5 4.7 maximum_bitcast_fusion
  257.2 8.8 copy.67
  266.0 2.9 broadcast_in_dim.59
  269.0 130.9 %scatter_fusion = f32[2,768,640]{2,0,1:T(2,128)} fusion(f32[2,768,640]{2,0,1:T(2,128)} %broadcast_in_dim.59, s32[1024]{0:T(1024)S(1)} %bitcast.212, f32[1024,2,640]{2,1,0:T(2,128)} %copy.67), kind=kCustom, calls=%fused_computation.4 | custom fusion | flops 1310720 | bytes 15732736 | tf_op jit(solution)/shard_map/scatter-add | solution.py:152
  399.9 1.8 fusion.82
  401.7 2.1 collective-permute-start.3
  403.8 22.7 %collective-permute-done.3 = bf16[2,256,640]{2,0,1:T(2,128)(2,1)S(1)} collective-permute-done((bf16[2,256,640]{2,0,1:T(2,128)(2,1)S(1)}, bf16[2,256,640]{2,0,1:T(2,128)(2,1)S(1)}, u32[]{:S(2)}, u32[]{:S(2)}) %collective-permute-start.3) | collective-permute-done | bytes 655392 | tf_op jit(solution)/shard_map/ppermute | solution.py:17
  426.5 2.0 fusion.67
  428.6 1.9 collective-permute-start.4
  430.5 1.0 pad_maximum_fusion.2
  431.5 1.2 copy.70
  432.8 25.8 %collective-permute-done.4 = bf16[2,256,640]{2,0,1:T(2,128)(2,1)S(1)} collective-permute-done((bf16[2,256,640]{2,0,1:T(2,128)(2,1)S(1)}, bf16[2,256,640]{2,0,1:T(2,128)(2,1)S(1)}, u32[]{:S(2)}, u32[]{:S(2)}) %collective-permute-start.4) | collective-permute-done | bytes 655392 | tf_op jit(solution)/shard_map/ppermute | solution.py:17
  458.6 2.0 fusion.65
  460.6 1.9 collective-permute-start.5
  462.5 1.3 dynamic-slice
  465.5 1057.3 %all-reduce.5.cloned.1.call-done = f32[2,128,640]{2,0,1:T(2,128)} async-done(((f32[2,128,640]{2,0,1:T(2,128)}), f32[2,128,640]{2,0,1:T(2,128)}) %all-reduce.5.cloned.1.call-update) | async-done | bytes 655376
  1523.5 1.6 convert_element_type.66
  1526.2 1.5 slice.113
  1527.9 32.8 %all-reduce.1 = (f32[256]{0:T(256)S(1)}, f32[256]{0:T(256)S(1)}) all-reduce(f32[256]{0:T(256)S(1)} %fusion.74, f32[256]{0:T(256)S(1)} %fusion.81), channel_id=1, replica_groups=mesh['ctx'=64,'head'=8] {'head'}, use_global_device_ids=true, to_apply=%region_11.12 | all-reduce | flops 512 | bytes 4096 | tf_op jit(solution)/shard_map/psum | solution.py:170
  1562.6 0.9 fusion.80
  (214 shorter events, 57.0 us)
Async XLA Ops:
  7.2 45.2 %copy-start = (bf16[256,640]{1,0:T(8,128)(2,1)S(1)}, bf16[256,640]{1,0:T(8,128)(2,1)}, u32[]{:S(2)}) copy-start(bf16[256,640]{1,0:T(8,128)(2,1)} %param.12) | copy-start | bytes 983044
  7.2 45.2 %copy-start.9 = (f32[640]{0:T(1024)S(1)}, f32[640]{0:T(1024)}, u32[]{:S(2)}) copy-start(f32[640]{0:T(1024)} %param.16) | copy-start | bytes 7684
  7.2 35.2 %copy-start.6 = (bf16[256,640]{1,0:T(8,128)(2,1)S(1)}, bf16[256,640]{1,0:T(8,128)(2,1)}, u32[]{:S(2)}) copy-start(bf16[256,640]{1,0:T(8,128)(2,1)} %param.13) | copy-start | bytes 983044
  7.2 43.8 %copy-start.21 = (s32[2,4]{1,0:T(2,128)S(1)}, s32[2,4]{1,0:T(2,128)}, u32[]{:S(2)}) copy-start(s32[2,4]{1,0:T(2,128)} %param.17) | copy-start | bytes 100
  7.2 43.9 %copy-start.22 = (s32[2]{0:T(128)S(1)}, s32[2]{0:T(128)}, u32[]{:S(2)}) copy-start(s32[2]{0:T(128)} %param.18) | copy-start | bytes 28
  8.4 58.3 %copy-start.2 = (bf16[256,640]{0,1:T(8,128)(2,1)}, bf16[256,640]{0,1:T(8,128)(2,1)S(1)}, u32[]{:S(2)}) copy-start(bf16[256,640]{0,1:T(8,128)(2,1)S(1)} %copy.54) | copy-start | bytes 983044
  9.7 57.1 %copy-start.10 = (f32[640]{0:T(1024)S(1)}, f32[640]{0:T(1024)}, u32[]{:S(2)}) copy-start(f32[640]{0:T(1024)} %param.15) | copy-start | bytes 7684
  41.2 11.9 copy-start.13
  41.2 25.7 %copy-start.15 = (f32[256]{0:T(256)}, f32[256]{0:T(256)S(1)}, u32[]{:S(2)}) copy-start(f32[256]{0:T(256)S(1)} %get-tuple-element.207) | copy-start | bytes 3076
  42.4 25.4 %copy-start.8 = (bf16[256,640]{1,0:T(8,128)(2,1)S(1)}, bf16[256,640]{1,0:T(8,128)(2,1)}, u32[]{:S(2)}) copy-start(bf16[256,640]{1,0:T(8,128)(2,1)} %param.14) | copy-start | bytes 983044
  42.5 22.3 %collective-permute-start = (bf16[2,256,640]{2,1,0:T(8,128)(2,1)S(1)}, bf16[2,256,640]{2,1,0:T(8,128)(2,1)S(1)}, u32[]{:S(2)}, u32[]{:S(2)}) collective-permute-start(bf16[2,256,640]{2,1,0:T(8,128)(2,1)S(1)} %pad_maximum_fusion.1), channel_id=1, source_target_pairs={{0,504},{8,0},{16,8},{24,16},{32,24},{40,32},{48,40},{56,48},{64,5... | collective-permute-start | bytes 1966088 | tf_op jit(solution)/shard_map/ppermute | solution.py:17
  51.2 0.6 copy-start.19
  53.1 49.8 %copy-start.23 = (s32[1,64]{1,0:T(1,128)S(1)}, s32[1,64]{1,0:T(1,128)}, u32[]{:S(2)}) copy-start(s32[1,64]{1,0:T(1,128)} %param.19) | copy-start | bytes 772
  54.0 50.0 %all-to-all-start = ((bf16[64,2,2,640]{3,2,1,0:T(2,128)(2,1)}), bf16[64,2,2,640]{3,2,1,0:T(2,128)(2,1)S(1)}, u32[]{:S(2)}, u32[]{:S(2)}) async-start(bf16[64,2,2,640]{3,2,1,0:T(2,128)(2,1)} %stack.24), calls=%async_computation | async-start | bytes 655360 | tf_op jit(solution)/shard_map/all_to_all | solution.py:49
  61.2 1461.6 %all-reduce.5.cloned.1.call-start = ((), (), s32[]{:S(2)}) async-start(), calls=%async_computation.1 | async-start | bytes 1310720
  64.8 36.0 %collective-permute-start.1 = (bf16[2,256,640]{2,1,0:T(8,128)(2,1)S(1)}, bf16[2,256,640]{2,1,0:T(8,128)(2,1)S(1)}, u32[]{:S(2)}, u32[]{:S(2)}) collective-permute-start(bf16[2,256,640]{2,1,0:T(8,128)(2,1)S(1)} %collective-permute-done), channel_id=1, source_target_pairs={{0,8},{8,16},{16,24},{24,32},{32,40},{40,48},{48,56},{56,64},{64,7... | collective-permute-start | bytes 1966088 | tf_op jit(solution)/shard_map/ppermute | solution.py:17
  100.8 34.0 %collective-permute-start.2 = (bf16[2,256,640]{2,1,0:T(8,128)(2,1)S(1)}, bf16[2,256,640]{2,1,0:T(8,128)(2,1)S(1)}, u32[]{:S(2)}, u32[]{:S(2)}) collective-permute-start(bf16[2,256,640]{2,1,0:T(8,128)(2,1)S(1)} %collective-permute-done.1), channel_id=1, source_target_pairs={{0,8},{8,16},{16,24},{24,32},{32,40},{40,48},{48,56},{56,64},{64,7... | collective-permute-start | bytes 1966088 | tf_op jit(solution)/shard_map/ppermute | solution.py:17
  157.4 4.0 copy-start.24
  167.1 5.7 copy-start.25
  172.7 4.0 copy-start.24
  182.3 5.6 copy-start.25
  188.0 4.0 copy-start.24
  197.6 5.7 copy-start.25
  203.2 4.0 copy-start.24
  212.9 5.7 copy-start.25
  218.5 4.0 copy-start.24
  228.1 5.7 copy-start.25
  266.0 2.9 copy-start.12
  399.9 30.6 %copy-start.7 = (f32[5,128,128]{1,2,0:T(8,128)S(1)}, f32[5,128,128]{1,2,0:T(8,128)}, u32[]{:S(2)}) copy-start(f32[5,128,128]{1,2,0:T(8,128)} %get-tuple-element.82) | copy-start | bytes 983044
  401.7 24.8 %collective-permute-start.3 = (bf16[2,256,640]{2,0,1:T(2,128)(2,1)S(1)}, bf16[2,256,640]{2,0,1:T(2,128)(2,1)S(1)}, u32[]{:S(2)}, u32[]{:S(2)}) collective-permute-start(bf16[2,256,640]{2,0,1:T(2,128)(2,1)S(1)} %fusion.82), channel_id=1, source_target_pairs={{0,8},{8,16},{16,24},{24,32},{32,40},{40,48},{48,56},{56,64},{64,7... | collective-permute-start | bytes 1966088 | tf_op jit(solution)/shard_map/ppermute | solution.py:17
  428.6 30.0 %collective-permute-start.4 = (bf16[2,256,640]{2,0,1:T(2,128)(2,1)S(1)}, bf16[2,256,640]{2,0,1:T(2,128)(2,1)S(1)}, u32[]{:S(2)}, u32[]{:S(2)}) collective-permute-start(bf16[2,256,640]{2,0,1:T(2,128)(2,1)S(1)} %fusion.67), channel_id=1, source_target_pairs={{0,8},{8,16},{16,24},{24,32},{32,40},{40,48},{48,56},{56,64},{64,7... | collective-permute-start | bytes 1966088 | tf_op jit(solution)/shard_map/ppermute | solution.py:17
  432.8 31.7 %copy-start.5 = (f32[5,2,128,128]{3,2,1,0:T(8,128)S(1)}, f32[5,2,128,128]{3,2,1,0:T(8,128)}, u32[]{:S(2)}) copy-start(f32[5,2,128,128]{3,2,1,0:T(8,128)} %get-tuple-element.79) | copy-start | bytes 1966084
  432.8 32.6 %copy-start.3 = (bf16[256,640]{0,1:T(8,128)(2,1)S(1)}, bf16[256,640]{0,1:T(8,128)(2,1)}, u32[]{:S(2)}) copy-start(bf16[256,640]{0,1:T(8,128)(2,1)} %copy-done.2) | copy-start | bytes 983044
  432.8 32.6 %copy-start.11 = (f32[640]{0:T(1024)S(1)}, f32[640]{0:T(1024)}, u32[]{:S(2)}) copy-start(f32[640]{0:T(1024)} %param.15) | copy-start | bytes 7684
  460.6 1063.0 %collective-permute-start.5 = (bf16[2,256,640]{2,0,1:T(2,128)(2,1)S(1)}, bf16[2,256,640]{2,0,1:T(2,128)(2,1)}, u32[]{:S(2)}, u32[]{:S(2)}) collective-permute-start(bf16[2,256,640]{2,0,1:T(2,128)(2,1)S(1)} %fusion.65), channel_id=1, source_target_pairs={{0,504},{8,0},{16,8},{24,16},{32,24},{40,32},{48,40},{56,48},{64,5... | collective-permute-start | bytes 1966088 | tf_op jit(solution)/shard_map/ppermute | solution.py:17
  464.4 1060.7 %copy-start.20 = (s32[2]{0:T(128)S(1)}, s32[2]{0:T(128)}, u32[]{:S(2)}) copy-start(s32[2]{0:T(128)} %copy-done.19) | copy-start | bytes 28
  1523.5 4.2 copy-start.1
  1525.1 35.7 %copy-start.16 = (f32[256]{0:T(256)S(1)}, f32[256]{0:T(256)}, u32[]{:S(2)}) copy-start(f32[256]{0:T(256)} %copy-done.15) | copy-start | bytes 3076
  1525.1 35.7 %copy-start.18 = (f32[256]{0:T(256)S(1)}, f32[256]{0:T(256)}, u32[]{:S(2)}) copy-start(f32[256]{0:T(256)} %get-tuple-element.208) | copy-start | bytes 3076
  1527.7 34.1 %copy-start.4 = (bf16[1,256,640]{2,0,1:T(2,128)(2,1)S(1)}, bf16[1,256,640]{2,0,1:T(2,128)(2,1)}, u32[]{:S(2)}) copy-start(bf16[1,256,640]{2,0,1:T(2,128)(2,1)} %slice.113) | copy-start | bytes 983044
  1527.7 34.9 %copy-start.14 = (f32[256]{0:T(256)S(1)}, f32[256]{0:T(256)}, u32[]{:S(2)}) copy-start(f32[256]{0:T(256)} %copy-done.13) | copy-start | bytes 3076
  1527.7 34.9 %copy-start.17 = (f32[256]{0:T(256)S(1)}, f32[256]{0:T(256)}, u32[]{:S(2)}) copy-start(f32[256]{0:T(256)} %get-tuple-element.203) | copy-start | bytes 3076
Sparse Core Ops, SparseCore 0:
  432.9 1089.8 all-reduce.4
